TPU v7x, 32 devices: a whole 2x2x4 slice. The times are simulated.
32 devices in a mesh: dp: 2 (over y), fsdp: 16 (over z, x, core).
Axes of the slice: x: 2, y: 2, z: 4, core: 2. Of those that a mesh axis runs over, the one named last changes fastest.
Arguments:
- tokens: bfloat16 [32768, 1024], P(('dp', 'fsdp')), may hold values from -12 to 12
- ln_gain: bfloat16 [1024], P(('dp', 'fsdp')), may hold values from 0.099609375 to 1.8984375
- ln_bias: bfloat16 [1024], P(('dp', 'fsdp')), may hold values from -1.75 to 1.75
- qkv_weight: bfloat16 [1024, 3072], P(('dp', 'fsdp')), may hold values from -0.1875 to 0.1875
- qkv_bias: bfloat16 [3072], P(('dp', 'fsdp')), may hold values from -1.75 to 1.75
- out_weight: bfloat16 [1024, 1024], P(('dp', 'fsdp')), may hold values from -0.75 to 0.75
- out_bias: bfloat16 [1024], P(('dp', 'fsdp')), may hold values from -1.75 to 1.75
- fc1_weight: bfloat16 [1024, 4096], P(('dp', 'fsdp')), may hold values from -0.1875 to 0.1875
- fc1_bias: bfloat16 [4096], P(('dp', 'fsdp')), may hold values from -3 to 3
- fc2_weight: bfloat16 [4096, 1024], P(('dp', 'fsdp')), may hold values from -0.09375 to 0.09375
- fc2_bias: bfloat16 [1024], P(('dp', 'fsdp')), may hold values from -1.75 to 1.75
- cotangent: float32 [32768, 1024], P(('dp', 'fsdp')), may hold values from -6 to 6
- doc_lengths: int32 [32, 4], P(('dp', 'fsdp')), may hold values from 1 to 512, 1024 in all within a row
- node_seeds: int32 [64, 64], replicated, may hold values from 0 to 1023
- node_weights: int32 [64], replicated, may hold values from 1 to 16
Outputs:
- output: float32 [32768, 1024], P(('dp', 'fsdp'))
- input_grad: float32 [32768, 1024], P(('dp', 'fsdp'))
- g_ln_gain: float32 [1024], P(('dp', 'fsdp'))
- g_ln_bias: float32 [1024], P(('dp', 'fsdp'))
- g_qkv_weight: float32 [1024, 3072], P(('dp', 'fsdp'))
- g_qkv_bias: float32 [3072], P(('dp', 'fsdp'))
- g_out_weight: float32 [1024, 1024], P(('dp', 'fsdp'))
- g_out_bias: float32 [1024], P(('dp', 'fsdp'))
- g_fc1_weight: float32 [1024, 4096], P(('dp', 'fsdp'))
- g_fc1_bias: float32 [4096], P(('dp', 'fsdp'))
- g_fc2_weight: float32 [4096, 1024], P(('dp', 'fsdp'))
- g_fc2_bias: float32 [1024], P(('dp', 'fsdp'))
Inputs may be any that keep to these rules, and one draw needn't show every extreme that they name: `doc_lengths`: each row holds the lengths of 4 documents that fill one sequence of 1024 tokens; its longest document has exactly 512 tokens.
All inputs are finite; a program needn't handle non-finite values.
Results may differ from a plain program's by a relative error of at most 0.0093.
Values may be sent and summed in bfloat16 or wider, within the bound.
No kernel may reach another device: no remote copies, remote signals or barrier semaphores. Data moves between devices by JAX's collectives and lax.ppermute only.
A program may use at most 256 MiB of HBM per device.

v0:
```python
import math
import jax
import jax.numpy as jnp
from jax import lax
from jax.sharding import PartitionSpec as P

D = 1024
HEADS = 16
HD = 64
ROT = 16
LEN = 1024
DOCS = 4
feature_scale = 0.2
epsilon = 1e-05
precise = lax.Precision.HIGHEST


def tables(node_seeds, node_weights):
    width = node_seeds.shape[1]
    uniform_pts = (node_seeds.astype(jnp.float32) + 0.5) / 1024.0
    nodes = math.sqrt(2.0) * lax.erf_inv(2.0 * uniform_pts - 1.0)
    order = jnp.arange(width).astype(jnp.float32)
    scales = jnp.where(order[:, None] == 0.0, math.sqrt(1.0 / width), math.sqrt(2.0 / width))
    basis = scales * jnp.cos(
        math.pi * (2.0 * order[None, :] + 1.0) * order[:, None] / (2.0 * width)
    )
    projection = jnp.dot(nodes, basis, precision=precise)
    weights_float = node_weights.astype(jnp.float32)
    return (projection, weights_float / jnp.sum(weights_float))


def layout(lengths):
    ends = jnp.cumsum(lengths)
    starts = ends - lengths
    places = jnp.arange(LEN, dtype=jnp.int32)
    doc_ids = jnp.sum((places[:, None] >= ends[None, :]).astype(jnp.int32), axis=1)
    owners = doc_ids[:, None] == jnp.arange(DOCS, dtype=jnp.int32)[None, :]
    begins = jnp.sum(jnp.where(owners, starts[None, :], 0), axis=1)
    return (doc_ids, (places - begins).astype(jnp.float32))


def rotary(positions):
    half_rot = ROT // 2
    freqs = 10000.0 ** (-2.0 * jnp.arange(half_rot).astype(jnp.float32) / ROT)
    angles = positions[:, None] * freqs[None, :]
    return (jnp.cos(angles), jnp.sin(angles))


def rotate(heads, cos_table, sin_table):
    half_rot = cos_table.shape[1]
    first = heads[..., :half_rot]
    second = heads[..., half_rot : 2 * half_rot]
    rest = heads[..., 2 * half_rot :]
    cos_wide = cos_table[:, None, :]
    sin_wide = sin_table[:, None, :]
    return jnp.concatenate(
        [first * cos_wide - second * sin_wide, second * cos_wide + first * sin_wide, rest], axis=-1
    )


def features(heads, cos_table, sin_table, projection):
    turned = feature_scale * rotate(heads, cos_table, sin_table)
    exponent = jnp.einsum("lhd,md->lhm", turned, projection, precision=precise)
    exponent = exponent - 0.5 * jnp.sum(turned * turned, axis=-1, keepdims=True)
    return jnp.exp(exponent)


def plain_dot(left, right):
    return jnp.dot(left, right, preferred_element_type=jnp.float32)


def outer_sum(left, right):
    return lax.dot_general(
        left, right, (((0,), (0,)), ((), ())), preferred_element_type=jnp.float32
    )


def back_proj(left, right):
    return lax.dot_general(
        left, right, (((1,), (1,)), ((), ())), preferred_element_type=jnp.float32
    )


def gelu_slope(upper):
    return 0.5 * (1.0 + lax.erf(upper / math.sqrt(2.0))) + upper * jnp.exp(
        -0.5 * upper * upper
    ) / math.sqrt(2.0 * math.pi)


def block_mask(doc_ids, first, block):
    places = jnp.arange(doc_ids.shape[0], dtype=jnp.int32)
    rows_here = places[first : first + block]
    same_doc = doc_ids[first : first + block, None] == doc_ids[None, :]
    return same_doc & (rows_here[:, None] >= places[None, :])


def attend(fq_low, fk_low, values_low, doc_ids):
    seq_len = doc_ids.shape[0]
    block = min(512, seq_len)
    outputs = []
    denoms = []
    for first in range(0, seq_len, block):
        mask = block_mask(doc_ids, first, block)
        raw = jnp.einsum(
            "qhm,khm->hqk",
            fq_low[first : first + block],
            fk_low,
            preferred_element_type=jnp.float32,
        )
        scores = jnp.where(mask[None], raw, 0.0)
        denom = jnp.sum(scores, axis=-1)
        numer = jnp.einsum(
            "hqk,khd->qhd",
            scores.astype(jnp.bfloat16),
            values_low,
            preferred_element_type=jnp.float32,
        )
        outputs.append(numer / denom.T[:, :, None])
        denoms.append(denom)
    return (jnp.concatenate(outputs, axis=0), jnp.concatenate(denoms, axis=1))


def attend_back(fq_low, fk_low, values_low, doc_ids, grad_out, attn_out, denom):
    seq_len = doc_ids.shape[0]
    block = min(512, seq_len)
    d_values = jnp.zeros(values_low.shape, jnp.float32)
    d_fk = jnp.zeros(fk_low.shape, jnp.float32)
    d_fq_parts = []
    for first in range(0, seq_len, block):
        mask = block_mask(doc_ids, first, block)
        fq_block = fq_low[first : first + block]
        raw = jnp.einsum("qhm,khm->hqk", fq_block, fk_low, preferred_element_type=jnp.float32)
        scores_low = jnp.where(mask[None], raw, 0.0).astype(jnp.bfloat16)
        den_block = denom[:, first : first + block].T
        grad_block = grad_out[first : first + block]
        d_num_low = (grad_block / den_block[:, :, None]).astype(jnp.bfloat16)
        d_denom = -jnp.sum(grad_block * attn_out[first : first + block], axis=-1) / den_block
        d_prod = jnp.einsum(
            "qhd,khd->hqk", d_num_low, values_low, preferred_element_type=jnp.float32
        )
        d_scores_low = jnp.where(
            mask[None],
            (d_prod + d_denom.T[:, :, None]).astype(jnp.bfloat16),
            jnp.zeros((), jnp.bfloat16),
        )
        d_values = d_values + jnp.einsum(
            "hqk,qhd->khd", scores_low, d_num_low, preferred_element_type=jnp.float32
        )
        d_fq_parts.append(
            jnp.einsum("hqk,khm->qhm", d_scores_low, fk_low, preferred_element_type=jnp.float32)
        )
        d_fk = d_fk + jnp.einsum(
            "hqk,qhm->khm", d_scores_low, fq_block, preferred_element_type=jnp.float32
        )
    return (jnp.concatenate(d_fq_parts, axis=0), d_fk, d_values)


def shards(
    tokens,
    ln_gain,
    ln_bias,
    qkv_weight,
    qkv_bias,
    out_weight,
    out_bias,
    fc1_weight,
    fc1_bias,
    fc2_weight,
    fc2_bias,
    cotangent,
    doc_lengths,
    node_seeds,
    node_weights,
):
    whole = (
        lax.all_gather(ln_gain, ("dp", "fsdp"), axis=0, tiled=True),
        lax.all_gather(ln_bias, ("dp", "fsdp"), axis=0, tiled=True),
        lax.all_gather(qkv_weight, ("dp", "fsdp"), axis=0, tiled=True),
        lax.all_gather(qkv_bias, ("dp", "fsdp"), axis=0, tiled=True),
        lax.all_gather(out_weight, ("dp", "fsdp"), axis=0, tiled=True),
        lax.all_gather(out_bias, ("dp", "fsdp"), axis=0, tiled=True),
        lax.all_gather(fc1_weight, ("dp", "fsdp"), axis=0, tiled=True),
        lax.all_gather(fc1_bias, ("dp", "fsdp"), axis=0, tiled=True),
        lax.all_gather(fc2_weight, ("dp", "fsdp"), axis=0, tiled=True),
        lax.all_gather(fc2_bias, ("dp", "fsdp"), axis=0, tiled=True),
    )
    (
        norm_gain,
        norm_shift,
        joint_weight,
        joint_bias,
        attn_weight,
        attn_bias,
        up_weight,
        up_bias,
        down_weight,
        down_bias,
    ) = whole
    rows_x = tokens.astype(jnp.float32)
    center = rows_x - jnp.mean(rows_x, axis=-1, keepdims=True)
    inv_std = lax.rsqrt(jnp.mean(center * center, axis=-1, keepdims=True) + epsilon)
    normed = center * inv_std
    hidden = normed * norm_gain.astype(jnp.float32) + norm_shift.astype(jnp.float32)
    hidden_low = hidden.astype(jnp.bfloat16)
    mixed = plain_dot(hidden_low, joint_weight) + joint_bias.astype(jnp.float32)
    upper = plain_dot(hidden_low, up_weight) + up_bias.astype(jnp.float32)
    act_low = jax.nn.gelu(upper, approximate=False).astype(jnp.bfloat16)
    branch_mlp = plain_dot(act_low, down_weight) + down_bias.astype(jnp.float32)
    projection, quad = tables(node_seeds, node_weights)
    seq = 0
    doc_ids, positions = layout(doc_lengths[seq])
    cos_table, sin_table = rotary(positions)
    query_heads = mixed[:, :D].reshape(LEN, HEADS, HD)
    key_heads = mixed[:, D : 2 * D].reshape(LEN, HEADS, HD)
    values_low = mixed[:, 2 * D :].reshape(LEN, HEADS, HD).astype(jnp.bfloat16)
    fq_low = (features(query_heads, cos_table, sin_table, projection) * quad).astype(jnp.bfloat16)
    fk_low = features(key_heads, cos_table, sin_table, projection).astype(jnp.bfloat16)
    attn_seq, denom = attend(fq_low, fk_low, values_low, doc_ids)
    kept = [
        (
            doc_ids,
            cos_table,
            sin_table,
            query_heads,
            key_heads,
            values_low,
            fq_low,
            fk_low,
            attn_seq,
            denom,
        )
    ]
    attn_parts = attn_seq.reshape(LEN, D)
    attn_low = attn_parts.astype(jnp.bfloat16)
    branch_attn = plain_dot(attn_low, attn_weight) + attn_bias.astype(jnp.float32)
    output = rows_x + branch_attn + branch_mlp
    again = (
        lax.all_gather(ln_gain, ("dp", "fsdp"), axis=0, tiled=True),
        lax.all_gather(ln_bias, ("dp", "fsdp"), axis=0, tiled=True),
        lax.all_gather(qkv_weight, ("dp", "fsdp"), axis=0, tiled=True),
        lax.all_gather(qkv_bias, ("dp", "fsdp"), axis=0, tiled=True),
        lax.all_gather(out_weight, ("dp", "fsdp"), axis=0, tiled=True),
        lax.all_gather(out_bias, ("dp", "fsdp"), axis=0, tiled=True),
        lax.all_gather(fc1_weight, ("dp", "fsdp"), axis=0, tiled=True),
        lax.all_gather(fc1_bias, ("dp", "fsdp"), axis=0, tiled=True),
        lax.all_gather(fc2_weight, ("dp", "fsdp"), axis=0, tiled=True),
        lax.all_gather(fc2_bias, ("dp", "fsdp"), axis=0, tiled=True),
    )
    (
        norm_gain,
        norm_shift,
        joint_weight,
        joint_bias,
        attn_weight,
        attn_bias,
        up_weight,
        up_bias,
        down_weight,
        down_bias,
    ) = again
    dy_low = cotangent.astype(jnp.bfloat16)
    dy_sums = jnp.sum(dy_low.astype(jnp.float32), axis=0)
    g_down_weight = outer_sum(act_low, dy_low)
    g_attn_weight = outer_sum(attn_low, dy_low)
    d_up_low = (back_proj(dy_low, down_weight) * gelu_slope(upper)).astype(jnp.bfloat16)
    g_up_weight = outer_sum(hidden_low, d_up_low)
    g_up_bias = jnp.sum(d_up_low.astype(jnp.float32), axis=0)
    d_attn = back_proj(dy_low, attn_weight)
    seq = 0
    (
        doc_ids,
        cos_table,
        sin_table,
        query_heads,
        key_heads,
        values_low,
        fq_low,
        fk_low,
        attn_seq,
        denom,
    ) = kept[seq]
    grad_out = d_attn.reshape(LEN, HEADS, HD)
    d_fq, d_fk, d_values = attend_back(
        fq_low, fk_low, values_low, doc_ids, grad_out, attn_seq, denom
    )

    def feature_pair(query_part, key_part):
        return (
            features(query_part, cos_table, sin_table, projection) * quad,
            features(key_part, cos_table, sin_table, projection),
        )

    unused, pull = jax.vjp(feature_pair, query_heads, key_heads)
    d_queries, d_keys = pull((d_fq, d_fk))
    d_mixed_parts = jnp.concatenate(
        [d_queries.reshape(LEN, D), d_keys.reshape(LEN, D), d_values.reshape(LEN, D)], axis=1
    )
    d_mixed_low = d_mixed_parts.astype(jnp.bfloat16)
    g_joint_weight = outer_sum(hidden_low, d_mixed_low)
    g_joint_bias = jnp.sum(d_mixed_low.astype(jnp.float32), axis=0)
    d_hidden = back_proj(d_mixed_low, joint_weight) + back_proj(d_up_low, up_weight)
    g_norm_gain = jnp.sum(d_hidden * normed, axis=0)
    g_norm_shift = jnp.sum(d_hidden, axis=0)
    d_normed = d_hidden * norm_gain.astype(jnp.float32)
    mean_grad = jnp.mean(d_normed, axis=-1, keepdims=True)
    mean_cross = jnp.mean(d_normed * normed, axis=-1, keepdims=True)
    input_grad = cotangent + inv_std * (d_normed - mean_grad - normed * mean_cross)
    reduced = (
        lax.psum_scatter(g_norm_gain, ("dp", "fsdp"), scatter_dimension=0, tiled=True),
        lax.psum_scatter(g_norm_shift, ("dp", "fsdp"), scatter_dimension=0, tiled=True),
        lax.psum_scatter(g_joint_weight, ("dp", "fsdp"), scatter_dimension=0, tiled=True),
        lax.psum_scatter(g_joint_bias, ("dp", "fsdp"), scatter_dimension=0, tiled=True),
        lax.psum_scatter(g_attn_weight, ("dp", "fsdp"), scatter_dimension=0, tiled=True),
        lax.psum_scatter(dy_sums, ("dp", "fsdp"), scatter_dimension=0, tiled=True),
        lax.psum_scatter(g_up_weight, ("dp", "fsdp"), scatter_dimension=0, tiled=True),
        lax.psum_scatter(g_up_bias, ("dp", "fsdp"), scatter_dimension=0, tiled=True),
        lax.psum_scatter(g_down_weight, ("dp", "fsdp"), scatter_dimension=0, tiled=True),
        lax.psum_scatter(dy_sums, ("dp", "fsdp"), scatter_dimension=0, tiled=True),
    )
    return (
        output,
        input_grad,
        reduced[0],
        reduced[1],
        reduced[2],
        reduced[3],
        reduced[4],
        reduced[5],
        reduced[6],
        reduced[7],
        reduced[8],
        reduced[9],
    )


def solution(mesh):
    in_specs = (
        P(("dp", "fsdp"), None),
        P(("dp", "fsdp")),
        P(("dp", "fsdp")),
        P(("dp", "fsdp"), None),
        P(("dp", "fsdp")),
        P(("dp", "fsdp"), None),
        P(("dp", "fsdp")),
        P(("dp", "fsdp"), None),
        P(("dp", "fsdp")),
        P(("dp", "fsdp"), None),
        P(("dp", "fsdp")),
        P(("dp", "fsdp"), None),
        P(("dp", "fsdp"), None),
        P(),
        P(),
    )
    out_specs = (
        P(("dp", "fsdp"), None),
        P(("dp", "fsdp"), None),
        P(("dp", "fsdp")),
        P(("dp", "fsdp")),
        P(("dp", "fsdp"), None),
        P(("dp", "fsdp")),
        P(("dp", "fsdp"), None),
        P(("dp", "fsdp")),
        P(("dp", "fsdp"), None),
        P(("dp", "fsdp")),
        P(("dp", "fsdp"), None),
        P(("dp", "fsdp")),
    )
    return jax.shard_map(shards, mesh=mesh, in_specs=in_specs, out_specs=out_specs, check_vma=False)
```

profile of v0, /device:TPU:4, one launch (start us, length us, event | category | flops | bytes accessed | tf_op | source)
XLA Modules:
  0.0 982.5 jit_solution(15464834726994419618)
XLA Ops:
  18.3 42.6 %all-reduce.17 = (bf16[3072]{0:T(1024)(128)(2,1)S(1)}, bf16[1024]{0:T(1024)(128)(2,1)S(1)}, bf16[1024]{0:T(1024)(128)(2,1)S(1)}, bf16[1024]{0:T(1024)(128)(2,1)}, bf16[1024]{0:T(1024)(128)(2,1)}) all-reduce(bf16[3072]{0:T(1024)(128)(2,1)S(1)} %dynamic-update-slice.2, ...), channel_id=1, replica_groups=mesh['dp'=2,'fsdp'=16] {'dp','fsdp'}, use_global_device_ids=true, to_apply=%add.8 | all-reduce | flops 7168 | bytes 28672
  78.0 62.4 %all-gather.6.cloned.1.call-done = bf16[1024,3072]{1,0:T(8,128)(2,1)} async-done(((bf16[32,3072]{1,0:T(8,128)(2,1)}), bf16[1024,3072]{1,0:T(8,128)(2,1)}) %all-gather.6.cloned.1.call-update) | async-done | bytes 6291472 | tf_op jit(solution)/shard_map/all_gather | solution.py:178
  140.4 9.0 broadcast_add_fusion
  175.9 6.8 fusion.44
  182.7 6.5 multiply_convert_fusion
  189.2 8.6 select_reduce_fusion
  197.8 8.7 select_reduce_fusion.1
  206.5 13.2 %bitcast_divide_fusion.1 = f32[512,16,64]{0,2,1:T(8,128)} fusion(bf16[1024,16,64]{0,2,1:T(8,128)(2,1)} %bitcast.93, bf16[16,512,1024]{2,1,0:T(8,128)(2,1)} %get-tuple-element.61, pred[512,1024]{1,0:T(8,128)(4,1)} %get-tuple-element.50, f32[512,16]{0,1:T(8,128)S(1)} %bitcast.104), kind=kOutput, calls=%fused_computation.87 | convolution fusion | flops 1082654720 | bytes 21528576 | tf_op jit(solution)/shard_map/hqk,khd->qhd/dot_general | solution.py:112
  219.7 11.8 %multiply_reduce_fusion.3 = (f32[512,16]{0,1:T(8,128)S(1)}, f32[512,16]{0,1:T(8,128)S(1)}, bf16[512,16,64]{0,2,1:T(8,128)(2,1)S(1)}, bf16[512,16,64]{0,2,1:T(8,128)(2,1)S(1)}) fusion(f32[1024,1024]{0,1:T(8,128)} %copy-done.21, f32[512,16,64]{0,2,1:T(8,128)} %bitcast_divide_fusion.1, f32[512,16]{0,1:T(8,128)S(1)} %bitcast.101, ...), kind=kOutput, calls=%fused_computation.88 | convolution fusion | flops 1085784064 | bytes 27885568 | tf_op jit(solution)/shard_map/hqk,khd->qhd/dot_general | solution.py:112
  238.2 11.5 %fusion.9 = bf16[16,512,1024]{2,1,0:T(8,128)(2,1)} fusion(f32[16,512]{1,0:T(8,128)S(1)} %bitcast_divide_fusion.3, pred[512,1024]{1,0:T(8,128)(4,1)} %get-tuple-element.50, bf16[1024,16,64]{0,2,1:T(8,128)(2,1)} %bitcast.95, f32[512,16,64]{0,2,1:T(8,128)} %bitcast.99, f32[512,16]{0,1:T(8,128)S(1)} %bitcast.105), kind=kOutput, calls=%fused_computation.17 | convolution fusion | flops 1099956224 | bytes 21561344 | tf_op jit(solution)/shard_map/qhd,khd->hqk/dot_general | solution.py:138
  249.7 10.8 %fusion.52 = f32[16,64,1024]{2,1,0:T(8,128)} fusion(bf16[16,512,1024]{2,1,0:T(8,128)(2,1)} %fusion.9, bf16[1024,16,64]{0,2,1:T(8,128)(2,1)S(1)} %copy-done.14), kind=kOutput, calls=%fused_computation.105 | convolution fusion | flops 1073741824 | bytes 22020096 | tf_op jit(solution)/shard_map/hqk,qhm->khm/dot_general | solution.py:152
  260.5 12.9 %convolution_bitcast_fusion.1 = f32[512,16,64]{0,2,1:T(8,128)} fusion(bf16[1024,16,64]{0,2,1:T(8,128)(2,1)} %copy-done.5, bf16[16,512,1024]{2,1,0:T(8,128)(2,1)} %fusion.9), kind=kOutput, calls=%fused_computation.100 | convolution fusion | flops 1073741824 | bytes 20971520 | tf_op jit(solution)/shard_map/hqk,khm->qhm/dot_general | solution.py:150
  273.5 11.3 %fusion.10 = bf16[16,512,1024]{2,1,0:T(8,128)(2,1)} fusion(f32[16,512]{1,0:T(8,128)S(1)} %bitcast_divide_fusion.2, pred[512,1024]{1,0:T(8,128)(4,1)} %get-tuple-element.51, bf16[1024,16,64]{0,2,1:T(8,128)(2,1)} %bitcast.96, f32[512,16,64]{0,2,1:T(8,128)} %bitcast.97, f32[512,16]{0,1:T(8,128)S(1)} %bitcast.102), kind=kOutput, calls=%fused_computation.18 | convolution fusion | flops 1099956224 | bytes 21561344 | tf_op jit(solution)/shard_map/qhd,khd->hqk/dot_general | solution.py:138
  284.9 8.4 fusion.183
  293.3 7.2 fusion.38
  302.5 13.0 %convolution_bitcast_fusion = f32[512,16,64]{0,2,1:T(8,128)} fusion(bf16[1024,16,64]{0,2,1:T(8,128)(2,1)} %copy-done.5, bf16[16,512,1024]{2,1,0:T(8,128)(2,1)} %fusion.10), kind=kOutput, calls=%fused_computation.99 | convolution fusion | flops 1073741824 | bytes 20971520 | tf_op jit(solution)/shard_map/hqk,khm->qhm/dot_general | solution.py:150
  321.5 6.9 fusion.39
  337.2 11.3 %fusion.18 = f32[16,64,1024]{2,1,0:T(8,128)} fusion(bf16[16,512,1024]{2,1,0:T(8,128)(2,1)} %get-tuple-element.61, pred[512,1024]{1,0:T(8,128)(4,1)S(1)} %copy-done.31, f32[512,16,64]{0,2,1:T(8,128)S(1)} %bitcast.100, f32[512,16]{0,1:T(8,128)S(1)} %bitcast.106), kind=kOutput, calls=%fused_computation.41 | convolution fusion | flops 1083179008 | bytes 23625728 | tf_op jit(solution)/shard_map/hqk,qhd->khd/dot_general | solution.py:146
  348.5 12.4 %add_convert_fusion.2 = bf16[16,64,1024]{2,1,0:T(8,128)(2,1)} fusion(f32[16,64,1024]{2,1,0:T(8,128)} %fusion.18, bf16[16,512,1024]{2,1,0:T(8,128)(2,1)} %get-tuple-element.59, pred[512,1024]{1,0:T(8,128)(4,1)S(1)} %copy-done.29, f32[512,16,64]{0,2,1:T(8,128)} %bitcast.98, f32[512,16]{0,1:T(8,128)S(1)} %bitcast.103), kind=kOutput, calls=%fused_computation.71 | convolution fusion | flops 1085276160 | bytes 25722880 | tf_op jit(solution)/shard_map/hqk,qhd->khd/dot_general | solution.py:146
  361.0 14.8 %fusion.172 = f32[1024,3072]{1,0:T(8,128)} fusion(bf16[1024,1024]{0,1:T(8,128)(2,1)} %bitcast.90, bf16[1024,1024]{0,1:T(8,128)(2,1)} %bitcast.82, bf16[1024,1024]{0,1:T(8,128)(2,1)} %bitcast.85, bf16[1024,1024]{1,0:T(8,128)(2,1)S(1)} %copy-done.7, f32[1024]{0:T(1024)S(1)} %copy-done.44, f32[1024]{0:T(1024)S(1)} %copy-done.41, f32[1024]{0:T(1024)S(1)} %copy-done.39, ...), kind=kOutput, calls=%fused_computation.256 | convolution fusion | flops 6467616768 | bytes 20987904 | tf_op jit(solution)/shard_map/dot_general | solution.py:73
  376.5 39.0 %all-gather = bf16[32,1,128]{2,1,0:T(2,128)(2,1)S(1)} all-gather(bf16[1,1,128]{2,1,0:T(2,128)(2,1)S(1)} %bitcast.109), channel_id=1, replica_groups=mesh['dp'=2,'fsdp'=16] {'dp','fsdp'}, dimensions={0}, use_global_device_ids=true | all-gather | bytes 8448 | tf_op jit(solution)/shard_map/all_gather | solution.py:183
  415.5 49.2 %fusion.2 = (bf16[1024,4096]{1,0:T(8,128)(2,1)S(1)}, f32[1024,4096]{1,0:T(8,128)}) fusion(f32[4096]{0:T(1024)S(1)} %bitcast.107, bf16[1024,4096]{1,0:T(8,128)(2,1)} %all-gather.10.cloned.1.call-done, bf16[1024,1024]{1,0:T(8,128)(2,1)S(1)} %copy-done.7, f32[1024]{0:T(1024)S(1)} %copy-done.44, f32[1024]{0:T(1024)S(1)} %copy-done.41, f32[1024]{0:T(1024)S(1)} %copy-done.39, ...), kind=kOutput, calls=%fused_computation.10 | convolution fusion | flops 8873050112 | bytes 35684352 | tf_op jit(solution)/shard_map/dot_general | solution.py:69
  468.0 11.9 %fusion.187 = f32[4096,1024]{1,0:T(8,128)} fusion(bf16[1024,4096]{1,0:T(8,128)(2,1)S(1)} %get-tuple-element.63, bf16[1024,1024]{1,0:T(8,128)(2,1)S(1)} %copy-done.26), kind=kOutput, calls=%fused_computation.267 | convolution fusion | flops 8589934592 | bytes 27262976 | tf_op jit(solution)/shard_map/dot_general | solution.py:73
  480.0 18.5 %convert_reduce_fusion = (f32[4096]{0:T(1024)S(1)}, bf16[1024,4096]{1,0:T(8,128)(2,1)S(1)}) fusion(f32[1024,4096]{1,0:T(8,128)} %get-tuple-element.64, f32[4096]{0:T(1024)S(1)} %bitcast.108, bf16[1024,1024]{1,0:T(8,128)(2,1)} %get-tuple-element.29, bf16[4096,1024]{1,0:T(8,128)(2,1)} %all-gather.12.cloned.1.call-done), kind=kOutput, calls=%fused_computation.19 | convolution fusion | flops 8644456448 | bytes 35684352 | tf_op jit(solution)/shard_map/dot_general | solution.py:79
  502.3 12.2 %fusion.174 = f32[1024,4096]{1,0:T(8,128)} fusion(bf16[1024,4096]{1,0:T(8,128)(2,1)S(1)} %get-tuple-element.69, bf16[1024,1024]{1,0:T(8,128)(2,1)S(1)} %copy-done.7, f32[1024]{0:T(1024)S(1)} %copy-done.44, f32[1024]{0:T(1024)S(1)} %copy-done.41, f32[1024]{0:T(1024)S(1)} %copy-done.39, f32[1024]{0:T(1024)S(1)} %copy-done.37), kind=kOutput, calls=%fused_computation.258 | convolution fusion | flops 8596226048 | bytes 27279360 | tf_op jit(solution)/shard_map/dot_general | solution.py:73
  524.7 9.6 fusion.173
  534.4 16.8 %fusion.34 = (f32[1024]{0:T(1024)S(1)}, f32[1024]{0:T(1024)S(1)}, f32[1024]{0:T(1024)S(1)}, f32[1024]{0:T(1024)S(1)}, f32[1024,1024]{1,0:T(8,128)}) fusion(bf16[1024,1024]{1,0:T(8,128)(2,1)S(1)} %copy-done.7, f32[1024]{0:T(1024)S(1)} %copy-done.39, f32[1024]{0:T(1024)S(1)} %copy-done.37, f32[1024]{0:T(1024)S(1)} %copy-done.41, ...), kind=kOutput, calls=%fused_computation.57 | convolution fusion | flops 8601464832 | bytes 27291648 | tf_op jit(solution)/shard_map/dot_general | solution.py:79
  551.1 39.7 %all-reduce.16 = (f32[1024]{0:T(1024)S(1)}, f32[1024]{0:T(1024)S(1)}, f32[3072]{0:T(1024)S(1)}, f32[1024]{0:T(1024)S(1)}, f32[4096]{0:T(1024)S(1)}) all-reduce(f32[1024]{0:T(1024)S(1)} %get-tuple-element.12, f32[1024]{0:T(1024)S(1)} %get-tuple-element.15, ...), channel_id=2, replica_groups=mesh['dp'=2,'fsdp'=16] {'dp','fsdp'}, use_global_device_ids=true, to_apply=%region_17.18.clone | all-reduce | flops 10240 | bytes 81920
  593.3 5.8 fusion.33
  599.2 15.1 %fusion.36 = f32[1024,1024]{1,0:T(8,128)} fusion(bf16[1024,1024]{1,0:T(8,128)(2,1)S(1)} %copy-done.7, f32[1024,1024]{1,0:T(8,128)S(1)} %copy-done.57, f32[1024]{0:T(1024)S(1)} %convert_element_type.135, f32[1024]{0:T(1024)S(1)} %convert_element_type.132, bf16[1024,4096]{1,0:T(8,128)(2,1)} %copy-done.58, bf16[4096,1024]{1,0:T(8,128)(2,1)} %all-gather.12.cloned.1.call-done), kind=kOutput, calls=%fused_computation.59 | convolution fusion | flops 8595177472 | bytes 27271168 | tf_op jit(solution)/shard_map/dot_general | solution.py:69
  614.3 173.4 %reduce-scatter.11.cloned.1.call-done = f32[128,1024]{1,0:T(8,128)} async-done(((f32[4096,1024]{1,0:T(8,128)}), f32[128,1024]{1,0:T(8,128)}) %reduce-scatter.11.cloned.1.call-update) | async-done | bytes 524304 | tf_op jit(solution)/shard_map/reduce_scatter | solution.py:317
  787.7 187.2 %reduce-scatter.9.cloned.1.call-done = f32[32,4096]{1,0:T(8,128)} async-done(((f32[1024,4096]{1,0:T(8,128)}), f32[32,4096]{1,0:T(8,128)}) %reduce-scatter.9.cloned.1.call-update) | async-done | bytes 524304 | tf_op jit(solution)/shard_map/reduce_scatter | solution.py:315
  (215 shorter events, 98.7 us)
Async XLA Ops:
  7.2 10.2 %copy-start.51 = (bf16[32]{0:T(256)(128)(2,1)S(1)}, bf16[32]{0:T(256)(128)(2,1)}, u32[]{:S(2)}) copy-start(bf16[32]{0:T(256)(128)(2,1)} %param.16) | copy-start | bytes 196
  7.2 10.4 %copy-start.52 = (bf16[32]{0:T(256)(128)(2,1)S(1)}, bf16[32]{0:T(256)(128)(2,1)}, u32[]{:S(2)}) copy-start(bf16[32]{0:T(256)(128)(2,1)} %param.17) | copy-start | bytes 196
  7.2 10.6 %copy-start.53 = (bf16[32]{0:T(256)(128)(2,1)S(1)}, bf16[32]{0:T(256)(128)(2,1)}, u32[]{:S(2)}) copy-start(bf16[32]{0:T(256)(128)(2,1)} %param.21) | copy-start | bytes 196
  7.2 10.9 %copy-start.54 = (bf16[96]{0:T(256)(128)(2,1)S(1)}, bf16[96]{0:T(256)(128)(2,1)}, u32[]{:S(2)}) copy-start(bf16[96]{0:T(256)(128)(2,1)} %param.19) | copy-start | bytes 580
  7.2 54.0 %copy-start.49 = (s32[64,64]{1,0:T(8,128)S(1)}, s32[64,64]{1,0:T(8,128)}, u32[]{:S(2)}) copy-start(s32[64,64]{1,0:T(8,128)} %param.28) | copy-start | bytes 49156
  7.3 61.4 %all-gather.8.cloned.1.call-start = ((), (), s32[]{:S(2)}) async-start(), calls=%async_computation.5 | async-start | bytes 2162688 | tf_op jit(solution)/shard_map/all_gather | solution.py:180
  8.0 132.4 %all-gather.6.cloned.1.call-start = ((), (), s32[]{:S(2)}) async-start(), calls=%async_computation.4 | async-start | bytes 6488064 | tf_op jit(solution)/shard_map/all_gather | solution.py:178
  8.7 406.8 %all-gather.10.cloned.1.call-start = ((), (), s32[]{:S(2)}) async-start(), calls=%async_computation.6 | async-start | bytes 8650752 | tf_op jit(solution)/shard_map/all_gather | solution.py:182
  9.5 470.6 %all-gather.12.cloned.1.call-start = ((), (), s32[]{:S(2)}) async-start(), calls=%async_computation.7 | async-start | bytes 8650752 | tf_op jit(solution)/shard_map/all_gather | solution.py:184
  10.0 604.3 %reduce-scatter.7.cloned.1.call-start = ((), (), s32[]{:S(2)}) async-start(), calls=%async_computation.9 | async-start | bytes 4325376 | tf_op jit(solution)/shard_map/reduce_scatter | solution.py:313
  16.3 124.0 %copy-start.36 = (f32[1024]{0:T(1024)}, f32[1024]{0:T(1024)S(1)}, u32[]{:S(2)}) copy-start(f32[1024]{0:T(1024)S(1)} %broadcast_multiply_fusion.4) | copy-start | bytes 12292
  17.1 123.3 %copy-start.38 = (f32[1024]{0:T(1024)}, f32[1024]{0:T(1024)S(1)}, u32[]{:S(2)}) copy-start(f32[1024]{0:T(1024)S(1)} %add_rsqrt_fusion) | copy-start | bytes 12292
  61.0 79.4 %copy-start.40 = (f32[1024]{0:T(1024)}, f32[1024]{0:T(1024)S(1)}, u32[]{:S(2)}) copy-start(f32[1024]{0:T(1024)S(1)} %convert_element_type.116) | copy-start | bytes 12292
  61.0 79.4 %copy-start.43 = (f32[1024]{0:T(1024)}, f32[1024]{0:T(1024)S(1)}, u32[]{:S(2)}) copy-start(f32[1024]{0:T(1024)S(1)} %convert_element_type.117) | copy-start | bytes 12292
  61.2 110.3 %copy-start.32 = (f32[1024,8]{0,1:T(8,128)}, f32[1024,8]{0,1:T(8,128)S(1)}, u32[]{:S(2)}) copy-start(f32[1024,8]{0,1:T(8,128)S(1)} %get-tuple-element.48) | copy-start | bytes 98308
  61.2 110.3 %copy-start.34 = (f32[1024,8]{0,1:T(8,128)}, f32[1024,8]{0,1:T(8,128)S(1)}, u32[]{:S(2)}) copy-start(f32[1024,8]{0,1:T(8,128)S(1)} %get-tuple-element.49) | copy-start | bytes 98308
  182.7 15.1 %copy-start.5 = (bf16[1024,16,64]{0,2,1:T(8,128)(2,1)}, bf16[1024,16,64]{0,2,1:T(8,128)(2,1)S(1)}, u32[]{:S(2)}) copy-start(bf16[1024,16,64]{0,2,1:T(8,128)(2,1)S(1)} %get-tuple-element.54) | copy-start | bytes 6291460
  238.2 11.5 %copy-start.14 = (bf16[1024,16,64]{0,2,1:T(8,128)(2,1)S(1)}, bf16[1024,16,64]{0,2,1:T(8,128)(2,1)}, u32[]{:S(2)}) copy-start(bf16[1024,16,64]{0,2,1:T(8,128)(2,1)} %copy-done.13) | copy-start | bytes 6291460
  273.5 340.8 %reduce-scatter.5.cloned.1.call-start = ((), (), s32[]{:S(2)}) async-start(), calls=%async_computation.8 | async-start | bytes 12976128 | tf_op jit(solution)/shard_map/reduce_scatter | solution.py:311
  273.5 11.4 %copy-start.3 = (f32[16,64,1024]{2,1,0:T(8,128)S(1)}, f32[16,64,1024]{2,1,0:T(8,128)}, u32[]{:S(2)}) copy-start(f32[16,64,1024]{2,1,0:T(8,128)} %fusion.52) | copy-start | bytes 12582916
  273.5 11.3 %copy-start.4 = (f32[1024,16,64]{0,2,1:T(8,128)S(1)}, f32[1024,16,64]{0,2,1:T(8,128)}, u32[]{:S(2)}) copy-start(f32[1024,16,64]{0,2,1:T(8,128)} %get-tuple-element.55) | copy-start | bytes 12582916
  337.2 11.3 %copy-start.29 = (pred[512,1024]{1,0:T(8,128)(4,1)S(1)}, pred[512,1024]{1,0:T(8,128)(4,1)}, u32[]{:S(2)}) copy-start(pred[512,1024]{1,0:T(8,128)(4,1)} %get-tuple-element.51) | copy-start | bytes 1572868
  348.5 12.5 %copy-start.7 = (bf16[1024,1024]{1,0:T(8,128)(2,1)S(1)}, bf16[1024,1024]{1,0:T(8,128)(2,1)}, u32[]{:S(2)}) copy-start(bf16[1024,1024]{1,0:T(8,128)(2,1)} %param.15) | copy-start | bytes 6291460
  348.5 12.5 %copy-start.37 = (f32[1024]{0:T(1024)S(1)}, f32[1024]{0:T(1024)}, u32[]{:S(2)}) copy-start(f32[1024]{0:T(1024)} %copy-done.36) | copy-start | bytes 12292
  348.5 12.5 %copy-start.39 = (f32[1024]{0:T(1024)S(1)}, f32[1024]{0:T(1024)}, u32[]{:S(2)}) copy-start(f32[1024]{0:T(1024)} %copy-done.38) | copy-start | bytes 12292
  348.5 12.5 %copy-start.41 = (f32[1024]{0:T(1024)S(1)}, f32[1024]{0:T(1024)}, u32[]{:S(2)}) copy-start(f32[1024]{0:T(1024)} %copy-done.40) | copy-start | bytes 12292
  348.5 12.5 %copy-start.44 = (f32[1024]{0:T(1024)S(1)}, f32[1024]{0:T(1024)}, u32[]{:S(2)}) copy-start(f32[1024]{0:T(1024)} %copy-done.43) | copy-start | bytes 12292
  375.9 411.8 %reduce-scatter.11.cloned.1.call-start = ((), (), s32[]{:S(2)}) async-start(), calls=%async_computation.11 | async-start | bytes 17301504 | tf_op jit(solution)/shard_map/reduce_scatter | solution.py:317
  415.5 52.5 %copy-start.26 = (bf16[1024,1024]{1,0:T(8,128)(2,1)S(1)}, bf16[1024,1024]{1,0:T(8,128)(2,1)}, u32[]{:S(2)}) copy-start(bf16[1024,1024]{1,0:T(8,128)(2,1)} %get-tuple-element.29) | copy-start | bytes 6291460
  480.0 494.9 %reduce-scatter.9.cloned.1.call-start = ((), (), s32[]{:S(2)}) async-start(), calls=%async_computation.10 | async-start | bytes 17301504 | tf_op jit(solution)/shard_map/reduce_scatter | solution.py:315
  534.4 16.8 %copy-start.42 = (f32[1024]{0:T(1024)S(1)}, f32[1024]{0:T(1024)}, u32[]{:S(2)}) copy-start(f32[1024]{0:T(1024)} %get-tuple-element.28) | copy-start | bytes 12292
  591.5 383.4 %copy-start.55 = (f32[32]{0:T(128)}, f32[32]{0:T(128)S(1)}, u32[]{:S(2)}) copy-start(f32[32]{0:T(128)S(1)} %dynamic-slice.3) | copy-start | bytes 388
  (37 other events, 171.9 us)
Sparse Core Ops, SparseCore 0:
  10.9 57.7 all-gather.7
  71.6 68.7 all-gather.5
  143.2 75.9 all-gather.9
  221.9 76.0 all-gather.11
  300.7 138.9 reduce-scatter.6
  446.2 153.8 reduce-scatter.4
  603.0 184.6 reduce-scatter.10
  790.7 184.1 reduce-scatter.8
where the time goes:
time: 986 us; the launch traced here: 982 us
  waiting for transfers between devices  426 us (43%)
  matrix products  332 us (34%)
  blocking collectives  121 us (12%)
  local copies, waits for them, and re-layouts  49.7 us (5%)
  other arithmetic  37.4 us (4%)
  between operations  15.2 us (2%)
    reduce_scatter x1, waiting for transfers between devices, shards(): lax.psum_scatter(g_up_weight, ('dp', 'fsdp'), scatter_dimension=0, tiled=...  187 us
    reduce_scatter x1, waiting for transfers between devices, shards(): lax.psum_scatter(g_down_weight, ('dp', 'fsdp'), scatter_dimension=0, tile...  173 us
    unnamed x2, blocking collectives  82.3 us
    dot_general x4, matrix products, plain_dot(): return jnp.dot(left, right, preferred_element_type=jnp.float32)  77.8 us
    all_gather x1, waiting for transfers between devices, shards(): lax.all_gather(qkv_weight, ('dp', 'fsdp'), axis=0, tiled=True)  62.4 us
    dot_general x4, matrix products, back_proj(): lax.dot_general(left, right, (((1,), (1,)), ((), ())), preferred_element_...  49.5 us
    dot_general x4, matrix products, outer_sum(): lax.dot_general(left, right, (((0,), (0,)), ((), ())), preferred_element_...  43.3 us
    all_gather x1, blocking collectives, shards(): lax.all_gather(fc1_bias, ('dp', 'fsdp'), axis=0, tiled=True)  39 us
  transfers between devices with their start and end apart: 8, of which 4 were waited for; matrix products, arithmetic and copies ran while one was open for 41% of the time, Pallas kernels for 0%

commit v1 on v0

--- a/solution.py
+++ b/solution.py
@@ -13,6 +13,28 @@
 feature_scale = 0.2
 epsilon = 1e-05
 precise = lax.Precision.HIGHEST
+
+
+def in_order(pieces, dim):
+    shape = list(pieces.shape[1:])
+    shape[dim] *= pieces.shape[0]
+    return jnp.moveaxis(pieces, 0, dim).reshape(shape)
+
+
+def grow_blocks(x, axis):
+    devices = lax.axis_size(axis)
+    blocks = x[None]
+    for level in range(devices.bit_length() - 1):
+        distance = 1 << level
+        received = lax.ppermute(blocks, axis, [(i, i ^ distance) for i in range(devices)])
+        both = jnp.stack([blocks, received])
+        upper = lax.axis_index(axis) >> level & 1
+        blocks = jnp.where(upper == 0, both, both[::-1]).reshape(-1, *x.shape)
+    return blocks
+
+
+def gather_by_bits(x, axis, dim):
+    return in_order(grow_blocks(x, axis), dim)
 
 
 def tables(node_seeds, node_weights):
@@ -175,7 +197,7 @@
     whole = (
         lax.all_gather(ln_gain, ("dp", "fsdp"), axis=0, tiled=True),
         lax.all_gather(ln_bias, ("dp", "fsdp"), axis=0, tiled=True),
-        lax.all_gather(qkv_weight, ("dp", "fsdp"), axis=0, tiled=True),
+        gather_by_bits(qkv_weight, ("dp", "fsdp"), 0),
         lax.all_gather(qkv_bias, ("dp", "fsdp"), axis=0, tiled=True),
         lax.all_gather(out_weight, ("dp", "fsdp"), axis=0, tiled=True),
         lax.all_gather(out_bias, ("dp", "fsdp"), axis=0, tiled=True),

time: 986 us -> 1070 us (1.085)
  blocking collectives: 121 us -> 179 us
  waiting for transfers between devices: 426 us -> 440 us
    ppermute x0 -> x5, waiting for transfers between devices: none -> 107 us  [grow_blocks(): lax.ppermute(blocks, axis, [(i, i ^ distance) for i in range(devices)])]
    all_gather x1, waiting for transfers between devices: 62.4 us -> 0.01 us  [shards(): lax.all_gather(qkv_weight, ('dp', 'fsdp'), axis=0, tiled=True)]
    unnamed x2, blocking collectives: 82.3 us -> 140 us
    reduce_scatter x1, waiting for transfers between devices: 173 us -> 142 us  [shards(): lax.psum_scatter(g_down_weight, ('dp', 'fsdp'), scatter_dimension=0, tile...]
  transfers between devices with their start and end apart: 8 -> 13, of which waited for: 4 -> 6; matrix products, arithmetic and copies ran while one was open for 41% -> 38% of each run, Pallas kernels for 0% -> 0%
where the time goes in v1:
time: 1070 us; the launch traced here: 1060 us
  waiting for transfers between devices  440 us (41%)
  matrix products  331 us (31%)
  blocking collectives  179 us (17%)
  local copies, waits for them, and re-layouts  47.7 us (4%)
  other arithmetic  44.8 us (4%)
  between operations  15.3 us (1%)
    reduce_scatter x1, waiting for transfers between devices, shards(): lax.psum_scatter(g_up_weight, ('dp', 'fsdp'), scatter_dimension=0, tiled=...  189 us
    reduce_scatter x1, waiting for transfers between devices, shards(): lax.psum_scatter(g_down_weight, ('dp', 'fsdp'), scatter_dimension=0, tile...  142 us
    unnamed x2, blocking collectives  140 us
    ppermute x5, waiting for transfers between devices, grow_blocks(): lax.ppermute(blocks, axis, [(i, i ^ distance) for i in range(devices)])  107 us
    dot_general x4, matrix products, plain_dot(): return jnp.dot(left, right, preferred_element_type=jnp.float32)  75.8 us
    dot_general x4, matrix products, back_proj(): lax.dot_general(left, right, (((1,), (1,)), ((), ())), preferred_element_...  49.8 us
    dot_general x4, matrix products, outer_sum(): lax.dot_general(left, right, (((0,), (0,)), ((), ())), preferred_element_...  43.3 us
    all_gather x1, blocking collectives, shards(): lax.all_gather(fc1_bias, ('dp', 'fsdp'), axis=0, tiled=True)  39.5 us
  transfers between devices with their start and end apart: 13, of which 6 were waited for; matrix products, arithmetic and copies ran while one was open for 38% of the time, Pallas kernels for 0%

profile of v1, /device:TPU:4, one launch (start us, length us, event | category | flops | bytes accessed | tf_op | source)
XLA Modules:
  0.0 1063.9 jit_solution(2204393974308437081)
XLA Ops:
  13.8 9.8 collective-permute-done.1
  25.7 19.9 %collective-permute-done.2 = bf16[4,32,3072]{2,1,0:T(8,128)(2,1)} collective-permute-done((bf16[4,32,3072]{2,1,0:T(8,128)(2,1)S(1)}, bf16[4,32,3072]{2,1,0:T(8,128)(2,1)}, u32[]{:S(2)}, u32[]{:S(2)}) %collective-permute-start.2) | collective-permute-done | bytes 786464 | tf_op jit(solution)/shard_map/ppermute | solution.py:29
  52.9 94.9 %all-reduce.17 = (bf16[3072]{0:T(1024)(128)(2,1)S(1)}, bf16[1024]{0:T(1024)(128)(2,1)S(1)}, bf16[1024]{0:T(1024)(128)(2,1)S(1)}, bf16[1024]{0:T(1024)(128)(2,1)}, bf16[1024]{0:T(1024)(128)(2,1)}) all-reduce(bf16[3072]{0:T(1024)(128)(2,1)S(1)} %dynamic-update-slice.2, ...), channel_id=1, replica_groups=mesh['dp'=2,'fsdp'=16] {'dp','fsdp'}, use_global_device_ids=true, to_apply=%add.8 | all-reduce | flops 7168 | bytes 28672
  167.8 76.1 %collective-permute-done.4 = bf16[16,32,3072]{2,1,0:T(8,128)(2,1)} collective-permute-done((bf16[16,32,3072]{2,1,0:T(8,128)(2,1)}, bf16[16,32,3072]{2,1,0:T(8,128)(2,1)}, u32[]{:S(2)}, u32[]{:S(2)}) %collective-permute-start.4) | collective-permute-done | bytes 3145760 | tf_op jit(solution)/shard_map/ppermute | solution.py:29
  249.2 6.9 broadcast_add_fusion
  289.0 6.5 multiply_convert_fusion
  295.6 8.7 select_reduce_fusion
  304.3 8.9 select_reduce_fusion.1
  313.2 13.2 %bitcast_divide_fusion.1 = f32[512,16,64]{0,2,1:T(8,128)} fusion(bf16[1024,16,64]{0,2,1:T(8,128)(2,1)} %bitcast.114, bf16[16,512,1024]{2,1,0:T(8,128)(2,1)} %get-tuple-element.63, pred[512,1024]{1,0:T(8,128)(4,1)} %get-tuple-element.52, f32[512,16]{0,1:T(8,128)S(1)} %bitcast.129), kind=kOutput, calls=%fused_computation.92 | convolution fusion | flops 1082654720 | bytes 21528576 | tf_op jit(solution)/shard_map/hqk,khd->qhd/dot_general | solution.py:134
  326.4 11.9 %multiply_reduce_fusion.3 = (f32[512,16]{0,1:T(8,128)S(1)}, f32[512,16]{0,1:T(8,128)S(1)}, bf16[512,16,64]{0,2,1:T(8,128)(2,1)S(1)}, bf16[512,16,64]{0,2,1:T(8,128)(2,1)S(1)}) fusion(f32[1024,1024]{0,1:T(8,128)} %copy-done.20, f32[512,16,64]{0,2,1:T(8,128)} %bitcast_divide_fusion.1, f32[512,16]{0,1:T(8,128)S(1)} %bitcast.126, ...), kind=kOutput, calls=%fused_computation.93 | convolution fusion | flops 1085784064 | bytes 27885568 | tf_op jit(solution)/shard_map/hqk,khd->qhd/dot_general | solution.py:134
  345.0 11.4 %fusion.9 = bf16[16,512,1024]{2,1,0:T(8,128)(2,1)} fusion(f32[16,512]{1,0:T(8,128)S(1)} %bitcast_divide_fusion.3, pred[512,1024]{1,0:T(8,128)(4,1)} %get-tuple-element.52, bf16[1024,16,64]{0,2,1:T(8,128)(2,1)} %bitcast.116, f32[512,16,64]{0,2,1:T(8,128)} %bitcast.120, f32[512,16]{0,1:T(8,128)S(1)} %bitcast.130), kind=kOutput, calls=%fused_computation.17 | convolution fusion | flops 1099956224 | bytes 21561344 | tf_op jit(solution)/shard_map/qhd,khd->hqk/dot_general | solution.py:160
  356.4 10.9 %fusion.52 = f32[16,64,1024]{2,1,0:T(8,128)} fusion(bf16[16,512,1024]{2,1,0:T(8,128)(2,1)} %fusion.9, bf16[1024,16,64]{0,2,1:T(8,128)(2,1)S(1)} %copy-done.15), kind=kOutput, calls=%fused_computation.112 | convolution fusion | flops 1073741824 | bytes 22020096 | tf_op jit(solution)/shard_map/hqk,qhm->khm/dot_general | solution.py:174
  367.3 13.2 %convolution_bitcast_fusion.1 = f32[512,16,64]{0,2,1:T(8,128)} fusion(bf16[1024,16,64]{0,2,1:T(8,128)(2,1)} %copy-done.5, bf16[16,512,1024]{2,1,0:T(8,128)(2,1)} %fusion.9), kind=kOutput, calls=%fused_computation.105 | convolution fusion | flops 1073741824 | bytes 20971520 | tf_op jit(solution)/shard_map/hqk,khm->qhm/dot_general | solution.py:172
  380.6 11.3 %fusion.10 = bf16[16,512,1024]{2,1,0:T(8,128)(2,1)} fusion(f32[16,512]{1,0:T(8,128)S(1)} %bitcast_divide_fusion.2, pred[512,1024]{1,0:T(8,128)(4,1)} %get-tuple-element.53, bf16[1024,16,64]{0,2,1:T(8,128)(2,1)} %bitcast.117, f32[512,16,64]{0,2,1:T(8,128)} %bitcast.118, f32[512,16]{0,1:T(8,128)S(1)} %bitcast.127), kind=kOutput, calls=%fused_computation.18 | convolution fusion | flops 1099956224 | bytes 21561344 | tf_op jit(solution)/shard_map/qhd,khd->hqk/dot_general | solution.py:160
  391.9 8.1 fusion.185
  400.0 7.2 fusion.38
  409.2 13.0 %convolution_bitcast_fusion = f32[512,16,64]{0,2,1:T(8,128)} fusion(bf16[1024,16,64]{0,2,1:T(8,128)(2,1)} %copy-done.5, bf16[16,512,1024]{2,1,0:T(8,128)(2,1)} %fusion.10), kind=kOutput, calls=%fused_computation.104 | convolution fusion | flops 1073741824 | bytes 20971520 | tf_op jit(solution)/shard_map/hqk,khm->qhm/dot_general | solution.py:172
  428.2 7.2 fusion.39
  444.2 11.3 %fusion.18 = f32[16,64,1024]{2,1,0:T(8,128)} fusion(bf16[16,512,1024]{2,1,0:T(8,128)(2,1)} %get-tuple-element.63, pred[512,1024]{1,0:T(8,128)(4,1)S(1)} %copy-done.29, f32[512,16,64]{0,2,1:T(8,128)S(1)} %bitcast.121, f32[512,16]{0,1:T(8,128)S(1)} %bitcast.131), kind=kOutput, calls=%fused_computation.43 | convolution fusion | flops 1083179008 | bytes 23625728 | tf_op jit(solution)/shard_map/hqk,qhd->khd/dot_general | solution.py:168
  455.5 12.4 %add_convert_fusion.2 = bf16[16,64,1024]{2,1,0:T(8,128)(2,1)} fusion(f32[16,64,1024]{2,1,0:T(8,128)} %fusion.18, bf16[16,512,1024]{2,1,0:T(8,128)(2,1)} %get-tuple-element.61, pred[512,1024]{1,0:T(8,128)(4,1)S(1)} %copy-done.27, f32[512,16,64]{0,2,1:T(8,128)} %bitcast.119, f32[512,16]{0,1:T(8,128)S(1)} %bitcast.128), kind=kOutput, calls=%fused_computation.74 | convolution fusion | flops 1085276160 | bytes 25722880 | tf_op jit(solution)/shard_map/hqk,qhd->khd/dot_general | solution.py:168
  467.9 14.8 %fusion.174 = f32[1024,3072]{1,0:T(8,128)} fusion(bf16[1024,1024]{0,1:T(8,128)(2,1)} %bitcast.111, bf16[1024,1024]{0,1:T(8,128)(2,1)} %bitcast.100, bf16[1024,1024]{0,1:T(8,128)(2,1)} %bitcast.103, bf16[1024,1024]{1,0:T(8,128)(2,1)S(1)} %copy-done.7, f32[1024]{0:T(1024)S(1)} %copy-done.42, f32[1024]{0:T(1024)S(1)} %copy-done.37, f32[1024]{0:T(1024)S(1)} %copy-done.39, ...), kind=kOutput, calls=%fused_computation.268 | convolution fusion | flops 6467616768 | bytes 20987904 | tf_op jit(solution)/shard_map/dot_general | solution.py:95
  483.4 39.5 %all-gather = bf16[32,1,128]{2,1,0:T(2,128)(2,1)S(1)} all-gather(bf16[1,1,128]{2,1,0:T(2,128)(2,1)S(1)} %bitcast.134), channel_id=1, replica_groups=mesh['dp'=2,'fsdp'=16] {'dp','fsdp'}, dimensions={0}, use_global_device_ids=true | all-gather | bytes 8448 | tf_op jit(solution)/shard_map/all_gather | solution.py:205
  522.9 49.1 %fusion.2 = (bf16[1024,4096]{1,0:T(8,128)(2,1)S(1)}, f32[1024,4096]{1,0:T(8,128)}) fusion(f32[4096]{0:T(1024)S(1)} %bitcast.132, bf16[1024,4096]{1,0:T(8,128)(2,1)} %all-gather.8.cloned.1.call-done, bf16[1024,1024]{1,0:T(8,128)(2,1)S(1)} %copy-done.7, f32[1024]{0:T(1024)S(1)} %copy-done.42, f32[1024]{0:T(1024)S(1)} %copy-done.37, f32[1024]{0:T(1024)S(1)} %copy-done.39, ...), kind=kOutput, calls=%fused_computation.10 | convolution fusion | flops 8873050112 | bytes 35684352 | tf_op jit(solution)/shard_map/dot_general | solution.py:91
  575.3 11.9 %fusion.189 = f32[4096,1024]{1,0:T(8,128)} fusion(bf16[1024,4096]{1,0:T(8,128)(2,1)S(1)} %get-tuple-element.65, bf16[1024,1024]{1,0:T(8,128)(2,1)S(1)} %copy-done.24), kind=kOutput, calls=%fused_computation.279 | convolution fusion | flops 8589934592 | bytes 27262976 | tf_op jit(solution)/shard_map/dot_general | solution.py:95
  587.3 18.1 %convert_reduce_fusion = (f32[4096]{0:T(1024)S(1)}, bf16[1024,4096]{1,0:T(8,128)(2,1)S(1)}) fusion(f32[1024,4096]{1,0:T(8,128)} %get-tuple-element.66, f32[4096]{0:T(1024)S(1)} %bitcast.133, bf16[1024,1024]{1,0:T(8,128)(2,1)} %get-tuple-element.29, bf16[4096,1024]{1,0:T(8,128)(2,1)} %all-gather.10.cloned.1.call-done), kind=kOutput, calls=%fused_computation.19 | convolution fusion | flops 8644456448 | bytes 35684352 | tf_op jit(solution)/shard_map/dot_general | solution.py:101
  608.7 12.2 %fusion.176 = f32[1024,4096]{1,0:T(8,128)} fusion(bf16[1024,4096]{1,0:T(8,128)(2,1)S(1)} %get-tuple-element.71, bf16[1024,1024]{1,0:T(8,128)(2,1)S(1)} %copy-done.7, f32[1024]{0:T(1024)S(1)} %copy-done.42, f32[1024]{0:T(1024)S(1)} %copy-done.37, f32[1024]{0:T(1024)S(1)} %copy-done.39, f32[1024]{0:T(1024)S(1)} %copy-done.35), kind=kOutput, calls=%fused_computation.270 | convolution fusion | flops 8596226048 | bytes 27279360 | tf_op jit(solution)/shard_map/dot_general | solution.py:95
  630.8 10.7 %fusion.175 = f32[1024,1024]{1,0:T(8,128)S(1)} fusion(bf16[1024,3072]{1,0:T(8,128)(2,1)} %all-gather.12.cloned.1.call-done, bf16[1024,1024]{0,1:T(8,128)(2,1)} %bitcast.113, bf16[1024,1024]{0,1:T(8,128)(2,1)} %bitcast.102, bf16[1024,1024]{0,1:T(8,128)(2,1)} %bitcast.105), kind=kOutput, calls=%fused_computation.269 | convolution fusion | flops 6461325312 | bytes 16777216 | tf_op jit(solution)/shard_map/dot_general | solution.py:101
  641.5 16.4 %fusion.34 = (f32[1024]{0:T(1024)S(1)}, f32[1024]{0:T(1024)S(1)}, f32[1024]{0:T(1024)S(1)}, f32[1024]{0:T(1024)S(1)}, f32[1024,1024]{1,0:T(8,128)}) fusion(bf16[1024,1024]{1,0:T(8,128)(2,1)S(1)} %copy-done.7, f32[1024]{0:T(1024)S(1)} %copy-done.39, f32[1024]{0:T(1024)S(1)} %copy-done.35, f32[1024]{0:T(1024)S(1)} %copy-done.37, ...), kind=kOutput, calls=%fused_computation.60 | convolution fusion | flops 8601464832 | bytes 27291648 | tf_op jit(solution)/shard_map/dot_general | solution.py:101
  657.9 44.7 %all-reduce.16 = (f32[1024]{0:T(1024)S(1)}, f32[1024]{0:T(1024)S(1)}, f32[3072]{0:T(1024)S(1)}, f32[1024]{0:T(1024)S(1)}, f32[4096]{0:T(1024)S(1)}) all-reduce(f32[1024]{0:T(1024)S(1)} %get-tuple-element.12, f32[1024]{0:T(1024)S(1)} %get-tuple-element.15, ...), channel_id=2, replica_groups=mesh['dp'=2,'fsdp'=16] {'dp','fsdp'}, use_global_device_ids=true, to_apply=%region_17.18.clone | all-reduce | flops 10240 | bytes 81920
  711.0 15.3 %fusion.36 = f32[1024,1024]{1,0:T(8,128)} fusion(bf16[1024,1024]{1,0:T(8,128)(2,1)S(1)} %copy-done.7, f32[1024,1024]{1,0:T(8,128)S(1)} %copy-done.57, f32[1024]{0:T(1024)S(1)} %convert_element_type.135, f32[1024]{0:T(1024)S(1)} %convert_element_type.132, bf16[1024,4096]{1,0:T(8,128)(2,1)} %copy-done.58, bf16[4096,1024]{1,0:T(8,128)(2,1)} %all-gather.10.cloned.1.call-done), kind=kOutput, calls=%fused_computation.62 | convolution fusion | flops 8595177472 | bytes 27271168 | tf_op jit(solution)/shard_map/dot_general | solution.py:91
  726.3 141.6 %reduce-scatter.11.cloned.1.call-done = f32[128,1024]{1,0:T(8,128)} async-done(((f32[4096,1024]{1,0:T(8,128)}), f32[128,1024]{1,0:T(8,128)}) %reduce-scatter.11.cloned.1.call-update) | async-done | bytes 524304 | tf_op jit(solution)/shard_map/reduce_scatter | solution.py:339
  867.9 188.5 %reduce-scatter.9.cloned.1.call-done = f32[32,4096]{1,0:T(8,128)} async-done(((f32[1024,4096]{1,0:T(8,128)}), f32[32,4096]{1,0:T(8,128)}) %reduce-scatter.9.cloned.1.call-update) | async-done | bytes 524304 | tf_op jit(solution)/shard_map/reduce_scatter | solution.py:337
  (235 shorter events, 123.2 us)
Async XLA Ops:
  7.2 153.0 %all-gather.6.cloned.1.call-start = ((), (), s32[]{:S(2)}) async-start(), calls=%async_computation.4 | async-start | bytes 2162688 | tf_op jit(solution)/shard_map/all_gather | solution.py:202
  7.9 515.0 %all-gather.8.cloned.1.call-start = ((), (), s32[]{:S(2)}) async-start(), calls=%async_computation.5 | async-start | bytes 8650752 | tf_op jit(solution)/shard_map/all_gather | solution.py:204
  8.7 578.6 %all-gather.10.cloned.1.call-start = ((), (), s32[]{:S(2)}) async-start(), calls=%async_computation.6 | async-start | bytes 8650752 | tf_op jit(solution)/shard_map/all_gather | solution.py:206
  9.4 621.4 %all-gather.12.cloned.1.call-start = ((), (), s32[]{:S(2)}) async-start(), calls=%async_computation.7 | async-start | bytes 6488064 | tf_op jit(solution)/shard_map/all_gather | solution.py:262
  9.4 1.7 collective-permute-start
  12.2 11.3 %collective-permute-start.1 = (bf16[2,32,3072]{2,1,0:T(8,128)(2,1)S(1)}, bf16[2,32,3072]{2,1,0:T(8,128)(2,1)S(1)}, u32[]{:S(2)}, u32[]{:S(2)}) collective-permute-start(bf16[2,32,3072]{2,1,0:T(8,128)(2,1)S(1)} %get-tuple-element.45), channel_id=1, source_target_pairs={{0,2},{1,3},{2,0},{3,1},{4,6},{5,7},{6,4},{7,5},{8,10},{9,11},{10,... | collective-permute-start | bytes 1179656 | tf_op jit(solution)/shard_map/ppermute | solution.py:29
  23.7 27.8 %copy-start.53 = (s32[1,4]{1,0:T(1,128)S(1)}, s32[1,4]{1,0:T(1,128)}, u32[]{:S(2)}) copy-start(s32[1,4]{1,0:T(1,128)} %param.27) | copy-start | bytes 52
  23.7 28.0 %copy-start.48 = (bf16[32]{0:T(256)(128)(2,1)S(1)}, bf16[32]{0:T(256)(128)(2,1)}, u32[]{:S(2)}) copy-start(bf16[32]{0:T(256)(128)(2,1)} %param.25) | copy-start | bytes 196
  23.7 28.2 %copy-start.49 = (bf16[32]{0:T(256)(128)(2,1)S(1)}, bf16[32]{0:T(256)(128)(2,1)}, u32[]{:S(2)}) copy-start(bf16[32]{0:T(256)(128)(2,1)} %param.16) | copy-start | bytes 196
  23.7 28.5 %copy-start.50 = (bf16[32]{0:T(256)(128)(2,1)S(1)}, bf16[32]{0:T(256)(128)(2,1)}, u32[]{:S(2)}) copy-start(bf16[32]{0:T(256)(128)(2,1)} %param.17) | copy-start | bytes 196
  23.7 28.7 %copy-start.51 = (bf16[32]{0:T(256)(128)(2,1)S(1)}, bf16[32]{0:T(256)(128)(2,1)}, u32[]{:S(2)}) copy-start(bf16[32]{0:T(256)(128)(2,1)} %param.21) | copy-start | bytes 196
  23.7 28.9 %copy-start.52 = (bf16[96]{0:T(256)(128)(2,1)S(1)}, bf16[96]{0:T(256)(128)(2,1)}, u32[]{:S(2)}) copy-start(bf16[96]{0:T(256)(128)(2,1)} %param.19) | copy-start | bytes 580
  23.7 124.1 %copy-start.54 = (s32[64]{0:T(128)S(1)}, s32[64]{0:T(128)}, u32[]{:S(2)}) copy-start(s32[64]{0:T(128)} %param.29) | copy-start | bytes 772
  23.7 124.9 %copy-start.47 = (s32[64,64]{1,0:T(8,128)S(1)}, s32[64,64]{1,0:T(8,128)}, u32[]{:S(2)}) copy-start(s32[64,64]{1,0:T(8,128)} %param.28) | copy-start | bytes 49156
  23.8 125.3 %copy-start.6 = (bf16[1024,1024]{1,0:T(8,128)(2,1)S(1)}, bf16[1024,1024]{1,0:T(8,128)(2,1)}, u32[]{:S(2)}) copy-start(bf16[1024,1024]{1,0:T(8,128)(2,1)} %param.15) | copy-start | bytes 6291460
  23.9 21.6 %collective-permute-start.2 = (bf16[4,32,3072]{2,1,0:T(8,128)(2,1)S(1)}, bf16[4,32,3072]{2,1,0:T(8,128)(2,1)}, u32[]{:S(2)}, u32[]{:S(2)}) collective-permute-start(bf16[4,32,3072]{2,1,0:T(8,128)(2,1)S(1)} %bitcast.107), channel_id=1, source_target_pairs={{0,4},{1,5},{2,6},{3,7},{4,0},{5,1},{6,2},{7,3},{8,12},{9,13},{10,... | collective-permute-start | bytes 2359304 | tf_op jit(solution)/shard_map/ppermute | solution.py:29
  48.3 101.8 %collective-permute-start.3 = (bf16[8,32,3072]{2,1,0:T(8,128)(2,1)}, bf16[8,32,3072]{2,1,0:T(8,128)(2,1)}, u32[]{:S(2)}, u32[]{:S(2)}) collective-permute-start(bf16[8,32,3072]{2,1,0:T(8,128)(2,1)} %bitcast.10), channel_id=1, source_target_pairs={{0,8},{1,9},{2,10},{3,11},{4,12},{5,13},{6,14},{7,15},{8,0},{9,1},... | collective-permute-start | bytes 4718600 | tf_op jit(solution)/shard_map/ppermute | solution.py:29
  51.4 674.9 %reduce-scatter.7.cloned.1.call-start = ((), (), s32[]{:S(2)}) async-start(), calls=%async_computation.9 | async-start | bytes 4325376 | tf_op jit(solution)/shard_map/reduce_scatter | solution.py:335
  147.8 101.4 %copy-start.36 = (f32[1024]{0:T(1024)}, f32[1024]{0:T(1024)S(1)}, u32[]{:S(2)}) copy-start(f32[1024]{0:T(1024)S(1)} %convert_element_type.116) | copy-start | bytes 12292
  147.8 101.4 %copy-start.41 = (f32[1024]{0:T(1024)}, f32[1024]{0:T(1024)S(1)}, u32[]{:S(2)}) copy-start(f32[1024]{0:T(1024)S(1)} %convert_element_type.117) | copy-start | bytes 12292
  154.7 89.2 %collective-permute-start.4 = (bf16[16,32,3072]{2,1,0:T(8,128)(2,1)}, bf16[16,32,3072]{2,1,0:T(8,128)(2,1)}, u32[]{:S(2)}, u32[]{:S(2)}) collective-permute-start(bf16[16,32,3072]{2,1,0:T(8,128)(2,1)} %bitcast.13), channel_id=1, source_target_pairs={{0,16},{1,17},{2,18},{3,19},{4,20},{5,21},{6,22},{7,23},{8,24},{9,... | collective-permute-start | bytes 9437192 | tf_op jit(solution)/shard_map/ppermute | solution.py:29
  154.7 94.5 %copy-start.34 = (f32[1024]{0:T(1024)}, f32[1024]{0:T(1024)S(1)}, u32[]{:S(2)}) copy-start(f32[1024]{0:T(1024)S(1)} %broadcast_multiply_fusion.4) | copy-start | bytes 12292
  155.4 93.8 %copy-start.38 = (f32[1024]{0:T(1024)}, f32[1024]{0:T(1024)S(1)}, u32[]{:S(2)}) copy-start(f32[1024]{0:T(1024)S(1)} %add_rsqrt_fusion) | copy-start | bytes 12292
  155.6 122.7 %copy-start.30 = (f32[1024,8]{0,1:T(8,128)}, f32[1024,8]{0,1:T(8,128)S(1)}, u32[]{:S(2)}) copy-start(f32[1024,8]{0,1:T(8,128)S(1)} %get-tuple-element.50) | copy-start | bytes 98308
  155.7 122.7 %copy-start.32 = (f32[1024,8]{0,1:T(8,128)}, f32[1024,8]{0,1:T(8,128)S(1)}, u32[]{:S(2)}) copy-start(f32[1024,8]{0,1:T(8,128)S(1)} %get-tuple-element.51) | copy-start | bytes 98308
  164.8 79.1 %copy-start.20 = (f32[1024,1024]{0,1:T(8,128)}, f32[1024,1024]{0,1:T(8,128)S(1)}, u32[]{:S(2)}) copy-start(f32[1024,1024]{0,1:T(8,128)S(1)} %fusion.187) | copy-start | bytes 12582916
  380.5 345.8 %reduce-scatter.5.cloned.1.call-start = ((), (), s32[]{:S(2)}) async-start(), calls=%async_computation.8 | async-start | bytes 12976128 | tf_op jit(solution)/shard_map/reduce_scatter | solution.py:333
  482.8 385.1 %reduce-scatter.11.cloned.1.call-start = ((), (), s32[]{:S(2)}) async-start(), calls=%async_computation.11 | async-start | bytes 17301504 | tf_op jit(solution)/shard_map/reduce_scatter | solution.py:339
  522.9 52.4 %copy-start.24 = (bf16[1024,1024]{1,0:T(8,128)(2,1)S(1)}, bf16[1024,1024]{1,0:T(8,128)(2,1)}, u32[]{:S(2)}) copy-start(bf16[1024,1024]{1,0:T(8,128)(2,1)} %get-tuple-element.29) | copy-start | bytes 6291460
  587.2 469.2 %reduce-scatter.9.cloned.1.call-start = ((), (), s32[]{:S(2)}) async-start(), calls=%async_computation.10 | async-start | bytes 17301504 | tf_op jit(solution)/shard_map/reduce_scatter | solution.py:337
  641.5 16.4 %copy-start.40 = (f32[1024]{0:T(1024)S(1)}, f32[1024]{0:T(1024)}, u32[]{:S(2)}) copy-start(f32[1024]{0:T(1024)} %get-tuple-element.28) | copy-start | bytes 12292
  703.3 353.1 %copy-start.55 = (f32[32]{0:T(128)}, f32[32]{0:T(128)S(1)}, u32[]{:S(2)}) copy-start(f32[32]{0:T(128)S(1)} %dynamic-slice.3) | copy-start | bytes 388
  (42 other events, 264.0 us)
Sparse Core Ops, SparseCore 0:
  10.8 115.0 all-gather.5
  128.8 95.0 all-gather.7
  226.7 77.9 all-gather.9
  307.5 68.0 all-gather.11
  380.6 140.6 reduce-scatter.6
  527.8 153.0 reduce-scatter.4
  683.8 184.0 reduce-scatter.10
  870.9 185.5 reduce-scatter.8
